TPU v7x, 256 devices: a whole 4x4x8 slice. The times are simulated.
256 devices in a mesh: ctx: 64 (over x_hi, y, z), tp: 4 (over x_lo, core).
Axes of the slice: x: 4 (x_hi: 2, x_lo: 2; x = x_hi * 2 + x_lo), y: 4, z: 8, core: 2. Of those that a mesh axis runs over, the one named last changes fastest.
Arguments:
- hidden: bfloat16 [16384, 2048], P('ctx', 'tp'), may hold values from -6 to 6
- norm_gain_a: float32 [2048], replicated, may hold values from 0.5 to 1.5
- in_weight_a: bfloat16 [3, 2048, 2048], P(None, 'ctx', 'tp'), may hold values from -0.125 to 0.125
- mr_filter: bfloat16 [128, 128], P('tp'), may hold values from -0.5 to 0.5
- out_weight_a: bfloat16 [2048, 2048], P('tp', 'ctx'), may hold values from -0.125 to 0.125
- norm_gain_b: float32 [2048], replicated, may hold values from 0.5 to 1.5
- in_weight_b: bfloat16 [3, 2048, 2048], P(None, 'ctx', 'tp'), may hold values from -0.125 to 0.125
- li_rate: float32 [128, 16], P('tp'), may hold values from 6.1035156e-06 to 0.0333333333
- li_residue: float32 [128, 16], P('tp'), may hold values from -3 to 3
- out_weight_b: bfloat16 [2048, 2048], P('tp', 'ctx'), may hold values from -0.125 to 0.125
Outputs:
- mixed: bfloat16 [16384, 2048], P('ctx', 'tp')
- gated_medium: bfloat16 [2048, 16384], P('tp', 'ctx')
- gated_long: bfloat16 [2048, 16384], P('tp', 'ctx')
All inputs are finite; a program needn't handle non-finite values.
Results may differ from a plain program's by a relative error of at most 0.02.
Values may be sent and summed in bfloat16 or wider, within the bound.
No kernel may reach another device: no remote copies, remote signals or barrier semaphores. Data moves between devices by JAX's collectives and lax.ppermute only.
A program may use at most 64 MiB of HBM per device.

v0:
```python
import jax
import jax.numpy as jnp
from jax import lax
from jax.sharding import Mesh
from jax.sharding import PartitionSpec as P

GROUP = 16
TAPS = 128
CTX = ("ctx_0", "ctx_1", "ctx_2")


def laid_out(blocks, dim):
    blocks = jnp.moveaxis(blocks, 0, dim)
    dims = blocks.shape
    return blocks.reshape(*dims[:dim], dims[dim] * dims[dim + 1], *dims[dim + 2 :])


def gather_in_order(shard, axes, order):
    blocks = shard[None]
    for k in order:
        blocks = lax.all_gather(blocks, axes[k], axis=0, tiled=True)
    current = [lax.axis_size(axes[k]) for k in reversed(order)]
    blocks = blocks.reshape(*current, *shard.shape)
    turned = sorted(range(len(order)), key=lambda place: order[len(order) - 1 - place])
    return blocks.transpose(*turned, *range(len(order), blocks.ndim)).reshape(-1, *shard.shape)


def gathered_by_axis(shard, axes, order, dim):
    return laid_out(gather_in_order(shard, axes, order), dim)


def passed_along(value, axis, steps):
    count = lax.axis_size(axis)
    initial, last = (max(0, -steps), min(count, count - steps))
    return lax.ppermute(value, axis, [(source, source + steps) for source in range(initial, last)])


def from_everyone(shard, axis):
    copies = jnp.broadcast_to(shard, (lax.axis_size(axis), *shard.shape))
    return lax.all_to_all(copies, axis, split_axis=0, concat_axis=0, tiled=True)


def collect(shard, axis, dim):
    return laid_out(from_everyone(shard, axis), dim)


def cut_along(shard, dim, peers):
    before, after = (shard.shape[:dim], shard.shape[dim + 1 :])
    return jnp.moveaxis(shard.reshape(*before, peers, -1, *after), dim, 0)


def sent_and_summed(shard, axis, dim):
    peers = lax.axis_size(axis)
    blocks = lax.all_to_all(cut_along(shard, dim, peers), axis, 0, 0, tiled=True)
    return jnp.sum(blocks.astype(jnp.float32), axis=0)


def normalize(values, gain):
    widened = values.astype(jnp.float32)
    factor = lax.rsqrt(jnp.mean(widened * widened, axis=1, keepdims=True) + 1e-06)
    return (widened * factor * gain).astype(jnp.bfloat16)


def layer_inputs(gathered, gain, weight):
    normed = normalize(gathered, gain)
    projected = jnp.einsum(
        "knc,tn->kct",
        gathered_by_axis(weight, CTX, (0, 1, 2), 1),
        normed,
        preferred_element_type=jnp.float32,
    )
    return (projected[1], (projected[0] * projected[2]).astype(jnp.bfloat16))


def out_project(gated, weight):
    return jnp.einsum(
        "ct,cn->tn",
        gated,
        lax.all_gather(weight, CTX, axis=1, tiled=True),
        preferred_element_type=jnp.float32,
    )


def toeplitz_rows(filters):
    group_count, tap_count = filters.shape
    padded_filter = jnp.concatenate(
        [
            jnp.zeros((group_count, 1), filters.dtype),
            filters[:, ::-1],
            jnp.zeros((group_count, tap_count), filters.dtype),
        ],
        axis=1,
    )
    tiled = jnp.tile(padded_filter, (1, tap_count))[:, : tap_count * 2 * tap_count]
    return tiled.reshape(group_count, tap_count, 2 * tap_count)


def medium_conv(medium_in, mr_filter):
    channels_here, tokens_here = medium_in.shape
    prior_rim = passed_along(medium_in[:, tokens_here - TAPS :], CTX, 1)
    extended = jnp.concatenate([prior_rim, medium_in], axis=1)
    group_count = channels_here // GROUP
    block_count = tokens_here // TAPS
    grouped = extended.reshape(group_count, GROUP, block_count + 1, TAPS)
    windows = jnp.concatenate([grouped[:, :, :-1], grouped[:, :, 1:]], axis=3)
    filter_rows = toeplitz_rows(mr_filter)
    result = jnp.einsum("gts,gkbs->gkbt", filter_rows, windows, preferred_element_type=jnp.float32)
    return result.reshape(channels_here, tokens_here)


def chain_blocks(earlier, latter):
    return (earlier[0] * latter[1] + latter[0], earlier[1] * latter[1])


def long_parts(values, decay_rates, residues):
    group_count, per_group, length = values.shape
    block_count = length // TAPS
    blocks = values.astype(jnp.float32).reshape(group_count, per_group, block_count, TAPS)
    offsets = jnp.arange(TAPS, dtype=jnp.float32)
    mode_weight = residues * jnp.sqrt(2.0 * decay_rates)
    impulse = jnp.einsum("gm,gmt->gt", mode_weight, jnp.exp(-decay_rates[:, :, None] * offsets))
    within_rows = toeplitz_rows(impulse)[:, :, TAPS:]
    within = jnp.einsum("gts,gkbs->gkbt", within_rows, blocks)
    to_end = jnp.exp(-decay_rates[:, :, None] * (TAPS - 1.0 - offsets))
    block_end = jnp.einsum("gms,gkbs->gkbm", to_end, blocks)
    block_decay = jnp.broadcast_to(jnp.exp(-decay_rates * TAPS)[:, None, None, :], block_end.shape)
    after_block, unused_decay = lax.associative_scan(chain_blocks, (block_end, block_decay), axis=2)
    entering = jnp.concatenate(
        [jnp.zeros_like(after_block[:, :, :1]), after_block[:, :, :-1]], axis=2
    )
    from_start = mode_weight[:, :, None] * jnp.exp(-decay_rates[:, :, None] * (offsets + 1.0))
    carried = jnp.einsum("gmt,gkbm->gkbt", from_start, entering)
    return ((within + carried).reshape(group_count, per_group, length), after_block[:, :, -1])


def per_device(
    hidden,
    norm_gain_a,
    in_weight_a,
    mr_filter,
    out_weight_a,
    norm_gain_b,
    in_weight_b,
    li_rate,
    li_residue,
    out_weight_b,
):
    gathered = collect(hidden, "tp", 1)
    first_gate, medium_in = layer_inputs(gathered, norm_gain_a, in_weight_a)
    medium = medium_conv(medium_in, mr_filter)
    gated_medium = (first_gate * medium).astype(jnp.bfloat16)
    first_partial = out_project(gated_medium, out_weight_a)
    first_summed = sent_and_summed(first_partial.astype(jnp.bfloat16), "tp", 1)
    after_a = (hidden.astype(jnp.float32) + first_summed).astype(jnp.bfloat16)
    gathered_next = collect(after_a, "tp", 1)
    second_gate, long_in = layer_inputs(gathered_next, norm_gain_b, in_weight_b)
    by_channel = lax.all_to_all(long_in, CTX, split_axis=0, concat_axis=1, tiled=True)
    channel_count, full_length = by_channel.shape
    groups_here = max(1, channel_count // GROUP)
    per_group = channel_count // groups_here
    first_group = lax.axis_index(CTX) * channel_count // GROUP
    rates_here = lax.dynamic_slice_in_dim(li_rate, first_group, groups_here, 0)
    residues_here = lax.dynamic_slice_in_dim(li_residue, first_group, groups_here, 0)
    long_whole, unused_end = long_parts(
        by_channel.reshape(groups_here, per_group, full_length), rates_here, residues_here
    )
    long_out = lax.all_to_all(
        long_whole.reshape(channel_count, full_length).astype(jnp.bfloat16),
        CTX,
        split_axis=1,
        concat_axis=0,
        tiled=True,
    ).astype(jnp.float32)
    gated_long = (second_gate * long_out).astype(jnp.bfloat16)
    second_partial = out_project(gated_long, out_weight_b)
    second_summed = sent_and_summed(second_partial.astype(jnp.bfloat16), "tp", 1)
    mixed = (after_a.astype(jnp.float32) + second_summed).astype(jnp.bfloat16)
    return (mixed, gated_medium, gated_long)


def solution(mesh):
    split = Mesh(mesh.devices.reshape(2, 4, 8, mesh.shape["tp"]), ("ctx_0", "ctx_1", "ctx_2", "tp"))
    in_specs = (
        P(CTX, "tp"),
        P(),
        P(None, CTX, "tp"),
        P("tp", None),
        P("tp", CTX),
        P(),
        P(None, CTX, "tp"),
        P("tp", None),
        P("tp", None),
        P("tp", CTX),
    )
    out_specs = (P(CTX, "tp"), P("tp", CTX), P("tp", CTX))
    return jax.shard_map(
        per_device, mesh=split, in_specs=in_specs, out_specs=out_specs, check_vma=False
    )
```

profile of v0, /device:TPU:1, one launch (start us, length us, event | category | flops | bytes accessed | tf_op | source)
XLA Modules:
  0.0 450.9 jit_solution(16483814376759491080)
XLA Ops:
  7.2 6.6 %all-gather = bf16[6,32,512]{2,1,0:T(8,128)(2,1)S(1)} all-gather(bf16[3,32,512]{2,1,0:T(8,128)(2,1)} %param.12), channel_id=2, replica_groups=mesh['ctx_0'=2,'ctx_1'=4,'ctx_2'=8,'tp'=4] {'ctx_0'}, dimensions={0}, use_global_device_ids=true | all-gather | bytes 294912 | tf_op jit(solution)/shard_map/all_gather | solution.py:21
  13.9 13.3 %all_gather.25 = bf16[8,3,32,512]{3,2,1,0:T(8,128)(2,1)} all-gather(bf16[2,3,32,512]{3,2,1,0:T(8,128)(2,1)S(1)} %bitcast.150), channel_id=1, replica_groups=mesh['ctx_0'=2,'ctx_1'=4,'ctx_2'=8,'tp'=4] {'ctx_1'}, dimensions={0}, use_global_device_ids=true | all-gather | bytes 983040 | tf_op jit(solution)/shard_map/all_gather | solution.py:21
  27.3 0.7 all-gather.9.cloned.1.call-update
  28.0 5.6 %all-gather.1 = bf16[6,32,512]{2,1,0:T(8,128)(2,1)S(1)} all-gather(bf16[3,32,512]{2,1,0:T(8,128)(2,1)S(1)} %copy-done.2), channel_id=3, replica_groups=mesh['ctx_0'=2,'ctx_1'=4,'ctx_2'=8,'tp'=4] {'ctx_0'}, dimensions={0}, use_global_device_ids=true | all-gather | bytes 294912 | tf_op jit(solution)/shard_map/all_gather | solution.py:21
  33.7 11.3 %all_gather.29 = bf16[8,3,32,512]{3,2,1,0:T(8,128)(2,1)} all-gather(bf16[2,3,32,512]{3,2,1,0:T(8,128)(2,1)S(1)} %bitcast.151), channel_id=1, replica_groups=mesh['ctx_0'=2,'ctx_1'=4,'ctx_2'=8,'tp'=4] {'ctx_1'}, dimensions={0}, use_global_device_ids=true | all-gather | bytes 983040 | tf_op jit(solution)/shard_map/all_gather | solution.py:21
  45.0 1.1 broadcast_in_dim.16
  46.1 12.8 %all-to-all-start = ((bf16[4,256,512]{2,1,0:T(8,128)(2,1)}), bf16[4,256,512]{2,1,0:T(8,128)(2,1)S(1)}, u32[]{:S(2)}, u32[]{:S(2)}) async-start(bf16[4,256,512]{2,1,0:T(8,128)(2,1)} %broadcast_in_dim.16), calls=%async_computation | async-start | bytes 2097152 | tf_op jit(solution)/shard_map/all_to_all | solution.py:40
  59.0 13.4 %all-to-all-done = bf16[4,256,512]{2,1,0:T(8,128)(2,1)S(1)} async-done(((bf16[4,256,512]{2,1,0:T(8,128)(2,1)}), bf16[4,256,512]{2,1,0:T(8,128)(2,1)S(1)}, u32[]{:S(2)}, u32[]{:S(2)}) %all-to-all-start) | async-done | bytes 1048608 | tf_op jit(solution)/shard_map/all_to_all | solution.py:40
  73.6 33.6 %all-gather.7.cloned.1.call-done = bf16[64,3,32,512]{3,2,1,0:T(8,128)(2,1)} async-done(((bf16[8,3,32,512]{3,2,1,0:T(8,128)(2,1)}), bf16[64,3,32,512]{3,2,1,0:T(8,128)(2,1)}) %all-gather.7.cloned.1.call-update) | async-done | bytes 6291472 | tf_op jit(solution)/shard_map/all_gather | solution.py:21
  107.2 3.6 copy.84
  110.8 1.8 convolution_bitcast_fusion.1
  112.7 1.4 collective-permute-start
  114.1 2.0 tile.20
  116.1 6.2 %tile.21 = bf16[32,32896]{1,0:T(8,128)(2,1)} reshape(bf16[32,128,257]{2,1,0:T(8,128)(2,1)} %tile.20) | data formatting | bytes 4210688 | tf_op jit(solution)/shard_map/tile | solution.py:94
  122.3 1.6 slice-done
  123.9 1.8 copy.111
  126.6 1.1 copy-done
  127.7 0.8 fusion.6
  129.1 95.2 %all-gather.9.cloned.1.call-done = bf16[512,2048]{0,1:T(8,128)(2,1)} async-done(((bf16[512,32]{0,1:T(8,128)(2,1)}), bf16[512,2048]{0,1:T(8,128)(2,1)}) %all-gather.9.cloned.1.call-update) | async-done | bytes 2097168 | tf_op jit(solution)/shard_map/all_gather | solution.py:79
  224.4 2.3 convolution_convert_fusion.1
  226.8 20.6 %all_to_all.43 = bf16[4,256,512]{2,1,0:T(8,128)(2,1)S(1)} all-to-all(bf16[4,256,512]{2,1,0:T(8,128)(2,1)S(1)} %bitcast.140), channel_id=1, replica_groups=mesh['ctx_0'=2,'ctx_1'=4,'ctx_2'=8,'tp'=4] {'tp'}, dimensions={0} | all-to-all | bytes 2097152 | tf_op jit(solution)/shard_map/all_to_all | solution.py:54
  247.7 1.1 broadcast_in_dim.20
  248.7 4.1 all-to-all-start.2
  253.7 47.3 %all-gather.11.cloned.1.call-done = bf16[64,3,32,512]{3,2,1,0:T(8,128)(2,1)} async-done(((bf16[8,3,32,512]{3,2,1,0:T(8,128)(2,1)}), bf16[64,3,32,512]{3,2,1,0:T(8,128)(2,1)}) %all-gather.11.cloned.1.call-update) | async-done | bytes 6291472 | tf_op jit(solution)/shard_map/all_gather | solution.py:21
  301.0 6.6 %copy.93 = bf16[2,4,8,3,32,512]{5,4,2,1,0,3:T(8,128)(2,1)} copy(bf16[2,4,8,3,32,512]{5,4,3,0,1,2:T(8,128)(2,1)} %bitcast.135) | data formatting | bytes 12582912 | tf_op jit(solution)/shard_map/transpose | solution.py:25
  308.8 4.6 %convolution_bitcast_fusion = f32[3,512,256]{1,2,0:T(8,128)S(1)} fusion(bf16[256,2048,1]{0,1,2:T(8,128)(2,1)S(1)} %bitcast.138, bf16[3,2048,512]{2,1,0:T(8,128)(2,1)} %bitcast.131), kind=kOutput, calls=%fused_computation.16 | convolution fusion | flops 1610612736 | bytes 8912896 | tf_op jit(solution)/shard_map/knc,tn->kct/dot_general | solution.py:66
  313.4 0.8 copy.95
  314.3 9.9 %all-to-all-start.3 = ((bf16[64,8,256]{2,1,0:T(8,128)(2,1)}), bf16[64,8,256]{2,1,0:T(8,128)(2,1)S(1)}, u32[]{:S(2)}, u32[]{:S(2)}) async-start(bf16[64,8,256]{2,1,0:T(8,128)(2,1)} %bitcast.25), calls=%async_computation.3 | async-start | bytes 524288 | tf_op jit(solution)/shard_map/all_to_all | solution.py:157
  325.6 11.8 %all-to-all-done.3 = bf16[64,8,256]{2,1,0:T(8,128)(2,1)S(1)} async-done(((bf16[64,8,256]{2,1,0:T(8,128)(2,1)}), bf16[64,8,256]{2,1,0:T(8,128)(2,1)S(1)}, u32[]{:S(2)}, u32[]{:S(2)}) %all-to-all-start.3) | async-done | bytes 262176 | tf_op jit(solution)/shard_map/all_to_all | solution.py:157
  337.7 1.2 slice.197
  338.9 1.2 slice.199
  344.5 1.1 slice.240
  349.5 0.7 pad.51
  350.2 0.8 pad.53
  351.2 0.8 pad.52
  352.2 1.1 pad.54
  353.2 1.1 pad.55
  354.3 1.6 pad.112
  356.1 1.6 pad.81
  358.6 18.9 %all_to_all.44 = bf16[8,64,256]{2,0,1:T(8,128)(2,1)S(1)} all-to-all(bf16[8,64,256]{2,0,1:T(8,128)(2,1)S(1)} %copy.97), channel_id=1, replica_groups=mesh['ctx_0'=2,'ctx_1'=4,'ctx_2'=8,'tp'=4] {'ctx_0','ctx_1','ctx_2'}, dimensions={1} | all-to-all | bytes 524288 | tf_op jit(solution)/shard_map/all_to_all | solution.py:167
  377.9 40.8 %all-gather.13.cloned.1.call-done = bf16[512,2048]{0,1:T(8,128)(2,1)} async-done(((bf16[512,32]{0,1:T(8,128)(2,1)}), bf16[512,2048]{0,1:T(8,128)(2,1)}) %all-gather.13.cloned.1.call-update) | async-done | bytes 2097168 | tf_op jit(solution)/shard_map/all_gather | solution.py:79
  418.7 2.3 convolution_convert_fusion
  421.0 1.1 copy.116
  422.1 7.9 %all-to-all-start.5 = ((bf16[4,256,512]{2,1,0:T(8,128)(2,1)}), bf16[4,256,512]{2,1,0:T(8,128)(2,1)S(1)}, u32[]{:S(2)}, u32[]{:S(2)}) async-start(bf16[4,256,512]{2,1,0:T(8,128)(2,1)} %bitcast.122), calls=%async_computation.5 | async-start | bytes 2097152 | tf_op jit(solution)/shard_map/all_to_all | solution.py:54
  430.0 0.8 copy.100
  430.8 0.8 copy.101
  431.6 11.8 %all-to-all-done.5 = bf16[4,256,512]{2,1,0:T(8,128)(2,1)S(1)} async-done(((bf16[4,256,512]{2,1,0:T(8,128)(2,1)}), bf16[4,256,512]{2,1,0:T(8,128)(2,1)S(1)}, u32[]{:S(2)}, u32[]{:S(2)}) %all-to-all-start.5) | async-done | bytes 1048608 | tf_op jit(solution)/shard_map/all_to_all | solution.py:54
  443.6 0.8 add_convert_fusion
  (126 shorter events, 17.1 us)
Async XLA Ops:
  7.2 20.8 %copy-start.2 = (bf16[3,32,512]{2,1,0:T(8,128)(2,1)S(1)}, bf16[3,32,512]{2,1,0:T(8,128)(2,1)}, u32[]{:S(2)}) copy-start(bf16[3,32,512]{2,1,0:T(8,128)(2,1)} %param.16) | copy-start | bytes 294916
  7.2 37.8 %copy-start.1 = (bf16[256,512]{1,0:T(8,128)(2,1)S(1)}, bf16[256,512]{1,0:T(8,128)(2,1)}, u32[]{:S(2)}) copy-start(bf16[256,512]{1,0:T(8,128)(2,1)} %param.10) | copy-start | bytes 786436
  7.2 100.0 %all-gather.7.cloned.1.call-start = ((), (), s32[]{:S(2)}) async-start(), calls=%async_computation.6 | async-start | bytes 7077888 | tf_op jit(solution)/shard_map/all_gather | solution.py:21
  27.2 197.1 %all-gather.9.cloned.1.call-start = ((), (), s32[]{:S(2)}) async-start(), calls=%async_computation.7 | async-start | bytes 2129920 | tf_op jit(solution)/shard_map/all_gather | solution.py:79
  28.0 273.0 %all-gather.11.cloned.1.call-start = ((), (), s32[]{:S(2)}) async-start(), calls=%async_computation.8 | async-start | bytes 7077888 | tf_op jit(solution)/shard_map/all_gather | solution.py:21
  45.0 13.9 %copy-start.3 = (f32[2048]{0:T(1024)S(1)}, f32[2048]{0:T(1024)}, u32[]{:S(2)}) copy-start(f32[2048]{0:T(1024)} %param.11) | copy-start | bytes 24580
  45.0 13.9 %copy-start.4 = (bf16[32,128]{1,0:T(8,128)(2,1)S(1)}, bf16[32,128]{1,0:T(8,128)(2,1)}, u32[]{:S(2)}) copy-start(bf16[32,128]{1,0:T(8,128)(2,1)} %param.13) | copy-start | bytes 24580
  46.1 26.3 %all-to-all-start = ((bf16[4,256,512]{2,1,0:T(8,128)(2,1)}), bf16[4,256,512]{2,1,0:T(8,128)(2,1)S(1)}, u32[]{:S(2)}, u32[]{:S(2)}) async-start(bf16[4,256,512]{2,1,0:T(8,128)(2,1)} %broadcast_in_dim.16), calls=%async_computation | async-start | bytes 2097152 | tf_op jit(solution)/shard_map/all_to_all | solution.py:40
  112.7 13.1 %collective-permute-start = (bf16[512,128]{0,1:T(8,128)(2,1)S(1)}, bf16[512,128]{0,1:T(8,128)(2,1)S(1)}, u32[]{:S(2)}, u32[]{:S(2)}) collective-permute-start(bf16[512,128]{0,1:T(8,128)(2,1)S(1)} %slice.245), channel_id=1, source_target_pairs={{0,4},{4,8},{8,12},{12,16},{16,20},{20,24},{24,28},{28,32},{32,36}... | collective-permute-start | bytes 393224 | tf_op jit(solution)/shard_map/ppermute | solution.py:35
  122.3 1.6 slice-start
  126.1 1.6 copy-start
  247.6 5.9 %copy-start.5 = (f32[2048]{0:T(1024)S(1)}, f32[2048]{0:T(1024)}, u32[]{:S(2)}) copy-start(f32[2048]{0:T(1024)} %param.15) | copy-start | bytes 24580
  247.6 5.9 %copy-start.6 = (f32[32,16]{0,1:T(8,128)S(1)}, f32[32,16]{0,1:T(8,128)}, u32[]{:S(2)}) copy-start(f32[32,16]{0,1:T(8,128)} %param.17) | copy-start | bytes 6148
  247.6 5.9 %copy-start.7 = (f32[32,16]{0,1:T(8,128)S(1)}, f32[32,16]{0,1:T(8,128)}, u32[]{:S(2)}) copy-start(f32[32,16]{0,1:T(8,128)} %param.18) | copy-start | bytes 6148
  248.7 58.8 %all-to-all-start.2 = ((bf16[4,256,512]{2,1,0:T(8,128)(2,1)}), bf16[4,256,512]{2,1,0:T(8,128)(2,1)S(1)}, u32[]{:S(2)}, u32[]{:S(2)}) async-start(bf16[4,256,512]{2,1,0:T(8,128)(2,1)} %broadcast_in_dim.20), calls=%async_computation.2 | async-start | bytes 2097152 | tf_op jit(solution)/shard_map/all_to_all | solution.py:40
  252.9 165.8 %all-gather.13.cloned.1.call-start = ((), (), s32[]{:S(2)}) async-start(), calls=%async_computation.9 | async-start | bytes 2129920 | tf_op jit(solution)/shard_map/all_gather | solution.py:79
  314.3 23.1 %all-to-all-start.3 = ((bf16[64,8,256]{2,1,0:T(8,128)(2,1)}), bf16[64,8,256]{2,1,0:T(8,128)(2,1)S(1)}, u32[]{:S(2)}, u32[]{:S(2)}) async-start(bf16[64,8,256]{2,1,0:T(8,128)(2,1)} %bitcast.25), calls=%async_computation.3 | async-start | bytes 524288 | tf_op jit(solution)/shard_map/all_to_all | solution.py:157
  422.1 21.4 %all-to-all-start.5 = ((bf16[4,256,512]{2,1,0:T(8,128)(2,1)}), bf16[4,256,512]{2,1,0:T(8,128)(2,1)S(1)}, u32[]{:S(2)}, u32[]{:S(2)}) async-start(bf16[4,256,512]{2,1,0:T(8,128)(2,1)} %bitcast.122), calls=%async_computation.5 | async-start | bytes 2097152 | tf_op jit(solution)/shard_map/all_to_all | solution.py:54
Sparse Core Ops, SparseCore 0:
  27.3 79.8 all-gather.6
  110.7 113.6 all-gather.8
  226.1 74.8 all-gather.10
  304.4 114.2 all-gather.12
where the time goes:
time: 452 us; the launch traced here: 451 us
  waiting for transfers between devices  255 us (56%)
  blocking collectives  76.5 us (17%)
  local copies, waits for them, and re-layouts  50.8 us (11%)
  starting transfers between devices  36.2 us (8%)
  between operations  14.5 us (3%)
  matrix products  12.8 us (3%)
  other arithmetic  4.99 us (1%)
    all_gather x2, waiting for transfers between devices, out_project(): lax.all_gather(weight, CTX, axis=1, tiled=True)  136 us
    all_gather x2, waiting for transfers between devices, gather_in_order(): blocks = lax.all_gather(blocks, axes[k], axis=0, tiled=True)  80.9 us
    all_gather x4, blocking collectives, gather_in_order(): blocks = lax.all_gather(blocks, axes[k], axis=0, tiled=True)  36.9 us
    all_to_all x1, blocking collectives, sent_and_summed(): lax.all_to_all(cut_along(shard, dim, peers), axis, 0, 0, tiled=True)  20.6 us
    all_to_all x1, blocking collectives, per_device(): lax.all_to_all(long_whole.reshape(channel_count, full_length).astype(jnp....  18.9 us
    all_to_all x2, starting transfers between devices, from_everyone(): return lax.all_to_all(copies, axis, split_axis=0, concat_axis=0, tiled=True)  16.9 us
    all_to_all x2, waiting for transfers between devices, from_everyone(): return lax.all_to_all(copies, axis, split_axis=0, concat_axis=0, tiled=True)  13.4 us
    all_to_all x1, waiting for transfers between devices, per_device(): lax.all_to_all(long_in, CTX, split_axis=0, concat_axis=1, tiled=True)  11.8 us
  transfers between devices with their start and end apart: 9, of which 7 were waited for; matrix products, arithmetic and copies ran while one was open for 14% of the time, Pallas kernels for 0%

commit v1 on v0

--- a/solution.py
+++ b/solution.py
@@ -1,3 +1,4 @@
+import functools
 import jax
 import jax.numpy as jnp
 from jax import lax
@@ -7,6 +8,21 @@
 GROUP = 16
 TAPS = 128
 CTX = ("ctx_0", "ctx_1", "ctx_2")
+
+
+def trails_choose(arr_in, across):
+    return jnp.concatenate(
+        lax.all_to_all(
+            jnp.stack([arr_in for _ in range(lax.axis_size(across))], axis=0),
+            axis_name=across,
+            split_axis=0,
+            concat_axis=0,
+        ),
+        axis=1,
+    )
+
+
+tracks_pair = functools.partial(trails_choose, across=CTX)
 
 
 def laid_out(blocks, dim):
@@ -73,12 +89,7 @@
 
 
 def out_project(gated, weight):
-    return jnp.einsum(
-        "ct,cn->tn",
-        gated,
-        lax.all_gather(weight, CTX, axis=1, tiled=True),
-        preferred_element_type=jnp.float32,
-    )
+    return jnp.einsum("ct,cn->tn", gated, tracks_pair(weight), preferred_element_type=jnp.float32)
 
 
 def toeplitz_rows(filters):

time: 452 us -> 500 us (1.11); the launches traced: 451 us -> 493 us
  waiting for transfers between devices: 255 us -> 148 us
  local copies, waits for them, and re-layouts: 50.8 us -> 133 us
  other arithmetic: 4.99 us -> 39.8 us
  blocking collectives: 76.5 us -> 98.2 us
  starting transfers between devices: 36.2 us -> 44.6 us
    all_gather x2 -> x0, waiting for transfers between devices: 136 us -> none  [out_project(): lax.all_gather(weight, CTX, axis=1, tiled=True)]
    all_to_all x0 -> x2, waiting for transfers between devices: none -> 44 us  [trails_choose(): lax.all_to_all(jnp.stack([arr_in for _ in range(lax.axis_size(across))],...]
    pad x10, local copies, waits for them, and re-layouts: 7.4 us -> 48.1 us  [long_parts(): lax.associative_scan(chain_blocks, (block_end, block_decay), axis=2)]
    all_to_all x0 -> x1, blocking collectives: none -> 25.5 us  [from_everyone(): return lax.all_to_all(copies, axis, split_axis=0, concat_axis=0, tiled=True)]
    slice x17, local copies, waits for them, and re-layouts: 7.44 us -> 27.2 us  [long_parts(): lax.associative_scan(chain_blocks, (block_end, block_decay), axis=2)]
    all_to_all x0 -> x2, starting transfers between devices: none -> 19.2 us  [trails_choose(): lax.all_to_all(jnp.stack([arr_in for _ in range(lax.axis_size(across))],...]
    all_to_all x2 -> x1, waiting for transfers between devices: 13.4 us -> 0.01 us  [from_everyone(): return lax.all_to_all(copies, axis, split_axis=0, concat_axis=0, tiled=True)]
    add x12, other arithmetic: 0.94 us -> 13.7 us  [chain_blocks(): return (earlier[0] * latter[1] + latter[0], earlier[1] * latter[1])]
  transfers between devices with their start and end apart: 9 -> 8, of which waited for: 7 -> 5; matrix products, arithmetic and copies ran while one was open for 14% -> 10% of each run, Pallas kernels for 0% -> 0%
where the time goes in v1:
time: 500 us; the launch traced here: 493 us
  waiting for transfers between devices  148 us (30%)
  local copies, waits for them, and re-layouts  133 us (27%)
  blocking collectives  98.2 us (20%)
  starting transfers between devices  44.6 us (9%)
  other arithmetic  39.8 us (8%)
  matrix products  15.1 us (3%)
  between operations  14.6 us (3%)
    all_gather x2, waiting for transfers between devices, gather_in_order(): blocks = lax.all_gather(blocks, axes[k], axis=0, tiled=True)  91.9 us
    pad x10, local copies, waits for them, and re-layouts, long_parts(): lax.associative_scan(chain_blocks, (block_end, block_decay), axis=2)  48.1 us
    all_to_all x2, waiting for transfers between devices, trails_choose(): lax.all_to_all(jnp.stack([arr_in for _ in range(lax.axis_size(across))],...  44 us
    all_gather x4, blocking collectives, gather_in_order(): blocks = lax.all_gather(blocks, axes[k], axis=0, tiled=True)  36.9 us
    slice x17, local copies, waits for them, and re-layouts, long_parts(): lax.associative_scan(chain_blocks, (block_end, block_decay), axis=2)  27.2 us
    all_to_all x1, blocking collectives, from_everyone(): return lax.all_to_all(copies, axis, split_axis=0, concat_axis=0, tiled=True)  25.5 us
    all_to_all x2, starting transfers between devices, trails_choose(): lax.all_to_all(jnp.stack([arr_in for _ in range(lax.axis_size(across))],...  19.2 us
    all_to_all x1, blocking collectives, per_device(): lax.all_to_all(long_whole.reshape(channel_count, full_length).astype(jnp....  18.3 us
  transfers between devices with their start and end apart: 8, of which 5 were waited for; matrix products, arithmetic and copies ran while one was open for 10% of the time, Pallas kernels for 0%

profile of v1, /device:TPU:1, one launch (start us, length us, event | category | flops | bytes accessed | tf_op | source)
XLA Modules:
  0.0 493.3 jit_solution(9241194101817750048)
XLA Ops:
  7.2 6.6 %all-gather = bf16[6,32,512]{2,1,0:T(8,128)(2,1)S(1)} all-gather(bf16[3,32,512]{2,1,0:T(8,128)(2,1)} %param.12), channel_id=2, replica_groups=mesh['ctx_0'=2,'ctx_1'=4,'ctx_2'=8,'tp'=4] {'ctx_0'}, dimensions={0}, use_global_device_ids=true | all-gather | bytes 294912 | tf_op jit(solution)/shard_map/all_gather | solution.py:37
  13.9 13.3 %all_gather.19 = bf16[8,3,32,512]{3,2,1,0:T(8,128)(2,1)} all-gather(bf16[2,3,32,512]{3,2,1,0:T(8,128)(2,1)S(1)} %bitcast.161), channel_id=1, replica_groups=mesh['ctx_0'=2,'ctx_1'=4,'ctx_2'=8,'tp'=4] {'ctx_1'}, dimensions={0}, use_global_device_ids=true | all-gather | bytes 983040 | tf_op jit(solution)/shard_map/all_gather | solution.py:37
  27.3 5.6 %all-gather.1 = bf16[6,32,512]{2,1,0:T(8,128)(2,1)S(1)} all-gather(bf16[3,32,512]{2,1,0:T(8,128)(2,1)S(1)} %copy-done.5), channel_id=3, replica_groups=mesh['ctx_0'=2,'ctx_1'=4,'ctx_2'=8,'tp'=4] {'ctx_0'}, dimensions={0}, use_global_device_ids=true | all-gather | bytes 294912 | tf_op jit(solution)/shard_map/all_gather | solution.py:37
  32.9 11.3 %all_gather.22 = bf16[8,3,32,512]{3,2,1,0:T(8,128)(2,1)} all-gather(bf16[2,3,32,512]{3,2,1,0:T(8,128)(2,1)S(1)} %bitcast.162), channel_id=1, replica_groups=mesh['ctx_0'=2,'ctx_1'=4,'ctx_2'=8,'tp'=4] {'ctx_1'}, dimensions={0}, use_global_device_ids=true | all-gather | bytes 983040 | tf_op jit(solution)/shard_map/all_gather | solution.py:37
  44.4 25.5 %all_to_all.53 = bf16[4,256,512]{2,1,0:T(8,128)(2,1)S(1)} all-to-all(bf16[4,256,512]{2,1,0:T(8,128)(2,1)S(1)} %broadcast_in_dim.16), channel_id=1, replica_groups=mesh['ctx_0'=2,'ctx_1'=4,'ctx_2'=8,'tp'=4] {'tp'}, dimensions={0} | all-to-all | bytes 2097152 | tf_op jit(solution)/shard_map/all_to_all | solution.py:56
  71.4 12.7 %all-to-all-start.1 = ((bf16[64,512,32]{1,2,0:T(8,128)(2,1)}), bf16[64,512,32]{1,2,0:T(8,128)(2,1)}, u32[]{:S(2)}, u32[]{:S(2)}) async-start(bf16[64,512,32]{1,2,0:T(8,128)(2,1)} %stack.4), calls=%async_computation.1 | async-start | bytes 4194304 | tf_op jit(solution)/shard_map/all_to_all | solution.py:15
  85.6 66.2 %all-gather.5.cloned.1.call-done = bf16[64,3,32,512]{3,2,1,0:T(8,128)(2,1)} async-done(((bf16[8,3,32,512]{3,2,1,0:T(8,128)(2,1)}), bf16[64,3,32,512]{3,2,1,0:T(8,128)(2,1)}) %all-gather.5.cloned.1.call-update) | async-done | bytes 6291472 | tf_op jit(solution)/shard_map/all_gather | solution.py:37
  151.7 3.6 copy.96
  155.3 1.8 convolution_bitcast_fusion.1
  158.6 2.0 tile.20
  160.6 6.2 %tile.21 = bf16[32,32896]{1,0:T(8,128)(2,1)} reshape(bf16[32,128,257]{2,1,0:T(8,128)(2,1)} %tile.20) | data formatting | bytes 4210688 | tf_op jit(solution)/shard_map/tile | solution.py:105
  168.4 1.8 copy.126
  174.0 2.4 convolution_convert_fusion.1
  176.5 17.5 %all_to_all.54 = bf16[4,256,512]{2,1,0:T(8,128)(2,1)S(1)} all-to-all(bf16[4,256,512]{2,1,0:T(8,128)(2,1)S(1)} %bitcast.150), channel_id=1, replica_groups=mesh['ctx_0'=2,'ctx_1'=4,'ctx_2'=8,'tp'=4] {'tp'}, dimensions={0} | all-to-all | bytes 2097152 | tf_op jit(solution)/shard_map/all_to_all | solution.py:70
  196.0 4.9 all-to-all-start.3
  201.1 25.7 %all-gather.7.cloned.1.call-done = bf16[64,3,32,512]{3,2,1,0:T(8,128)(2,1)} async-done(((bf16[8,3,32,512]{3,2,1,0:T(8,128)(2,1)}), bf16[64,3,32,512]{3,2,1,0:T(8,128)(2,1)}) %all-gather.7.cloned.1.call-update) | async-done | bytes 6291472 | tf_op jit(solution)/shard_map/all_gather | solution.py:37
  226.8 6.5 %copy.105 = bf16[2,4,8,3,32,512]{5,4,2,1,0,3:T(8,128)(2,1)} copy(bf16[2,4,8,3,32,512]{5,4,3,0,1,2:T(8,128)(2,1)} %bitcast.144) | data formatting | bytes 12582912 | tf_op jit(solution)/shard_map/transpose | solution.py:41
  235.5 4.6 convolution_bitcast_fusion
  241.0 9.9 %all-to-all-start.4 = ((bf16[64,8,256]{2,1,0:T(8,128)(2,1)}), bf16[64,8,256]{2,1,0:T(8,128)(2,1)S(1)}, u32[]{:S(2)}, u32[]{:S(2)}) async-start(bf16[64,8,256]{2,1,0:T(8,128)(2,1)} %bitcast.160), calls=%async_computation.4 | async-start | bytes 524288 | tf_op jit(solution)/shard_map/all_to_all | solution.py:168
  257.6 6.3 %all-to-all-done.4 = bf16[64,8,256]{2,1,0:T(8,128)(2,1)S(1)} async-done(((bf16[64,8,256]{2,1,0:T(8,128)(2,1)}), bf16[64,8,256]{2,1,0:T(8,128)(2,1)S(1)}, u32[]{:S(2)}, u32[]{:S(2)}) %all-to-all-start.4) | async-done | bytes 262176 | tf_op jit(solution)/shard_map/all_to_all | solution.py:168
  266.5 1.8 slice.197
  268.3 1.8 slice.199
  275.1 1.8 slice.205
  276.9 1.8 slice.207
  281.9 1.7 slice.211
  294.6 1.7 fusion.53
  300.2 1.8 slice.234
  303.2 1.8 slice.240
  306.6 4.9 pad.46
  311.5 4.9 pad.47
  317.9 4.9 pad.49
  325.3 4.9 pad.48
  334.3 4.9 %pad.50 = f32[1,8,16,16]{2,3,1,0:T(8,128)} pad(f32[1,8,8,16]{2,3,1,0:T(8,128)} %pad_maximum_fusion.3, f32[]{:T(128)} %constant.21.clone.1), padding=0_0_0x0_0_0x0_1_1x0_0_0 | pad | bytes 12292 | tf_op jit(solution)/shard_map/pad | solution.py:138
  339.2 4.9 %pad.51 = f32[1,8,16,16]{2,3,1,0:T(8,128)} pad(f32[1,8,8,16]{2,3,1,0:T(8,128)} %add.154, f32[]{:T(128)} %constant.21.clone.1), padding=0_0_0x0_0_0x1_0_1x0_0_0 | pad | bytes 12292 | tf_op jit(solution)/shard_map/pad | solution.py:138
  345.7 5.0 %pad.53 = f32[1,8,32,16]{2,3,1,0:T(8,128)} pad(f32[1,8,16,16]{2,3,1,0:T(8,128)} %add.156, f32[]{:T(128)} %constant.21.clone.1), padding=0_0_0x0_0_0x1_0_1x0_0_0 | pad | bytes 24580 | tf_op jit(solution)/shard_map/pad | solution.py:138
  353.2 5.0 %pad.52 = f32[1,8,32,16]{2,3,1,0:T(8,128)} pad(f32[1,8,16,16]{2,3,1,0:T(8,128)} %pad_maximum_fusion.4, f32[]{:T(128)} %constant.21.clone.1), padding=0_0_0x0_0_0x0_1_1x0_0_0 | pad | bytes 24580 | tf_op jit(solution)/shard_map/pad | solution.py:138
  361.5 3.4 pad.54
  364.9 5.2 %pad.55 = f32[1,8,64,16]{2,3,1,0:T(8,128)} pad(f32[1,8,32,16]{2,3,1,0:T(8,128)} %add.158, f32[]{:T(128)} %constant.21.clone.1), padding=0_0_0x0_0_0x1_0_1x0_0_0 | pad | bytes 49156 | tf_op jit(solution)/shard_map/pad | solution.py:138
  371.5 5.4 %pad.112 = f32[1,8,128,16]{2,3,1,0:T(8,128)} pad(f32[1,8,64,16]{2,3,1,0:T(8,128)} %add.160, f32[]{:T(128)} %constant.21.clone.1), padding=0_0_0x0_0_0x1_0_1x0_0_0 | pad | bytes 98308
  384.4 18.3 %all_to_all.55 = bf16[8,64,256]{2,0,1:T(8,128)(2,1)S(1)} all-to-all(bf16[8,64,256]{2,0,1:T(8,128)(2,1)S(1)} %copy.109), channel_id=1, replica_groups=mesh['ctx_0'=2,'ctx_1'=4,'ctx_2'=8,'tp'=4] {'ctx_0','ctx_1','ctx_2'}, dimensions={1} | all-to-all | bytes 524288 | tf_op jit(solution)/shard_map/all_to_all | solution.py:178
  404.2 6.4 %all-to-all-start.6 = ((bf16[64,512,32]{1,2,0:T(8,128)(2,1)}), bf16[64,512,32]{1,2,0:T(8,128)(2,1)}, u32[]{:S(2)}, u32[]{:S(2)}) async-start(bf16[64,512,32]{1,2,0:T(8,128)(2,1)} %stack.5), calls=%async_computation.6 | async-start | bytes 4194304 | tf_op jit(solution)/shard_map/all_to_all | solution.py:15
  411.7 2.0 copy.110
  413.8 44.0 %all-to-all-done.6 = bf16[64,512,32]{1,2,0:T(8,128)(2,1)} async-done(((bf16[64,512,32]{1,2,0:T(8,128)(2,1)}), bf16[64,512,32]{1,2,0:T(8,128)(2,1)}, u32[]{:S(2)}, u32[]{:S(2)}) %all-to-all-start.6) | async-done | bytes 2097184 | tf_op jit(solution)/shard_map/all_to_all | solution.py:15
  457.8 2.5 convolution_convert_fusion
  461.4 9.3 %all-to-all-start.7 = ((bf16[4,256,512]{2,1,0:T(8,128)(2,1)}), bf16[4,256,512]{2,1,0:T(8,128)(2,1)}, u32[]{:S(2)}, u32[]{:S(2)}) async-start(bf16[4,256,512]{2,1,0:T(8,128)(2,1)} %bitcast.149), calls=%async_computation.7 | async-start | bytes 2097152 | tf_op jit(solution)/shard_map/all_to_all | solution.py:70
  470.7 1.9 copy.133
  472.6 2.1 copy.113
  478.8 5.4 %all-to-all-done.7 = bf16[4,256,512]{2,1,0:T(8,128)(2,1)} async-done(((bf16[4,256,512]{2,1,0:T(8,128)(2,1)}), bf16[4,256,512]{2,1,0:T(8,128)(2,1)}, u32[]{:S(2)}, u32[]{:S(2)}) %all-to-all-start.7) | async-done | bytes 1048608 | tf_op jit(solution)/shard_map/all_to_all | solution.py:70
  (148 shorter events, 84.7 us)
Async XLA Ops:
  7.2 20.1 %copy-start.5 = (bf16[3,32,512]{2,1,0:T(8,128)(2,1)S(1)}, bf16[3,32,512]{2,1,0:T(8,128)(2,1)}, u32[]{:S(2)}) copy-start(bf16[3,32,512]{2,1,0:T(8,128)(2,1)} %param.16) | copy-start | bytes 294916
  7.2 37.1 %copy-start.4 = (bf16[256,512]{1,0:T(8,128)(2,1)S(1)}, bf16[256,512]{1,0:T(8,128)(2,1)}, u32[]{:S(2)}) copy-start(bf16[256,512]{1,0:T(8,128)(2,1)} %param.10) | copy-start | bytes 786436
  7.2 144.5 %all-gather.5.cloned.1.call-start = ((), (), s32[]{:S(2)}) async-start(), calls=%async_computation.8 | async-start | bytes 7077888 | tf_op jit(solution)/shard_map/all_gather | solution.py:37
  27.2 199.6 %all-gather.7.cloned.1.call-start = ((), (), s32[]{:S(2)}) async-start(), calls=%async_computation.9 | async-start | bytes 7077888 | tf_op jit(solution)/shard_map/all_gather | solution.py:37
  44.2 25.6 %copy-start.6 = (bf16[512,32]{0,1:T(8,128)(2,1)S(1)}, bf16[512,32]{0,1:T(8,128)(2,1)}, u32[]{:S(2)}) copy-start(bf16[512,32]{0,1:T(8,128)(2,1)} %param.14) | copy-start | bytes 98308
  71.4 12.8 %copy-start.8 = (f32[2048]{0:T(1024)S(1)}, f32[2048]{0:T(1024)}, u32[]{:S(2)}) copy-start(f32[2048]{0:T(1024)} %param.11) | copy-start | bytes 24580
  71.4 12.8 %copy-start.9 = (bf16[32,128]{1,0:T(8,128)(2,1)S(1)}, bf16[32,128]{1,0:T(8,128)(2,1)}, u32[]{:S(2)}) copy-start(bf16[32,128]{1,0:T(8,128)(2,1)} %param.13) | copy-start | bytes 24580
  71.4 102.5 %all-to-all-start.1 = ((bf16[64,512,32]{1,2,0:T(8,128)(2,1)}), bf16[64,512,32]{1,2,0:T(8,128)(2,1)}, u32[]{:S(2)}, u32[]{:S(2)}) async-start(bf16[64,512,32]{1,2,0:T(8,128)(2,1)} %stack.4), calls=%async_computation.1 | async-start | bytes 4194304 | tf_op jit(solution)/shard_map/all_to_all | solution.py:15
  157.2 13.0 %collective-permute-start = (bf16[512,128]{0,1:T(8,128)(2,1)S(1)}, bf16[512,128]{0,1:T(8,128)(2,1)S(1)}, u32[]{:S(2)}, u32[]{:S(2)}) collective-permute-start(bf16[512,128]{0,1:T(8,128)(2,1)S(1)} %slice.245), channel_id=1, source_target_pairs={{0,4},{4,8},{8,12},{12,16},{16,20},{20,24},{24,28},{28,32},{32,36}... | collective-permute-start | bytes 393224 | tf_op jit(solution)/shard_map/ppermute | solution.py:51
  166.8 1.6 slice-start
  170.6 1.6 copy-start
  173.3 3.0 copy-start.1
  194.1 6.7 %copy-start.10 = (f32[2048]{0:T(1024)S(1)}, f32[2048]{0:T(1024)}, u32[]{:S(2)}) copy-start(f32[2048]{0:T(1024)} %param.15) | copy-start | bytes 24580
  194.1 6.7 %copy-start.11 = (f32[32,16]{0,1:T(8,128)S(1)}, f32[32,16]{0,1:T(8,128)}, u32[]{:S(2)}) copy-start(f32[32,16]{0,1:T(8,128)} %param.17) | copy-start | bytes 6148
  194.1 6.7 %copy-start.12 = (f32[32,16]{0,1:T(8,128)S(1)}, f32[32,16]{0,1:T(8,128)}, u32[]{:S(2)}) copy-start(f32[32,16]{0,1:T(8,128)} %param.18) | copy-start | bytes 6148
  194.2 0.7 copy-start.2
  196.0 37.4 %all-to-all-start.3 = ((bf16[4,256,512]{2,1,0:T(8,128)(2,1)}), bf16[4,256,512]{2,1,0:T(8,128)(2,1)}, u32[]{:S(2)}, u32[]{:S(2)}) async-start(bf16[4,256,512]{2,1,0:T(8,128)(2,1)} %broadcast_in_dim.20), calls=%async_computation.3 | async-start | bytes 2097152 | tf_op jit(solution)/shard_map/all_to_all | solution.py:56
  201.1 50.9 %copy-start.15 = (f32[16]{0:T(128)}, f32[16]{0:T(128)S(1)}, u32[]{:S(2)}) copy-start(f32[16]{0:T(128)S(1)} %get-tuple-element.19) | copy-start | bytes 196
  201.1 50.9 %copy-start.17 = (f32[16]{0:T(128)}, f32[16]{0:T(128)S(1)}, u32[]{:S(2)}) copy-start(f32[16]{0:T(128)S(1)} %get-tuple-element.20) | copy-start | bytes 196
  241.0 22.9 %all-to-all-start.4 = ((bf16[64,8,256]{2,1,0:T(8,128)(2,1)}), bf16[64,8,256]{2,1,0:T(8,128)(2,1)S(1)}, u32[]{:S(2)}, u32[]{:S(2)}) async-start(bf16[64,8,256]{2,1,0:T(8,128)(2,1)} %bitcast.160), calls=%async_computation.4 | async-start | bytes 524288 | tf_op jit(solution)/shard_map/all_to_all | solution.py:168
  251.5 0.8 copy-start.14
  255.6 28.0 %copy-start.13 = (f32[16]{0:T(128)S(1)}, f32[16]{0:T(128)}, u32[]{:S(2)}) copy-start(f32[16]{0:T(128)} %get-tuple-element.32) | copy-start | bytes 196
  332.7 48.7 %copy-start.16 = (f32[16]{0:T(128)S(1)}, f32[16]{0:T(128)}, u32[]{:S(2)}) copy-start(f32[16]{0:T(128)} %copy-done.15) | copy-start | bytes 196
  379.6 23.1 %copy-start.7 = (bf16[512,32]{0,1:T(8,128)(2,1)S(1)}, bf16[512,32]{0,1:T(8,128)(2,1)}, u32[]{:S(2)}) copy-start(bf16[512,32]{0,1:T(8,128)(2,1)} %param.19) | copy-start | bytes 98308
  404.2 53.6 %all-to-all-start.6 = ((bf16[64,512,32]{1,2,0:T(8,128)(2,1)}), bf16[64,512,32]{1,2,0:T(8,128)(2,1)}, u32[]{:S(2)}, u32[]{:S(2)}) async-start(bf16[64,512,32]{1,2,0:T(8,128)(2,1)} %stack.5), calls=%async_computation.6 | async-start | bytes 4194304 | tf_op jit(solution)/shard_map/all_to_all | solution.py:15
  461.4 22.9 %all-to-all-start.7 = ((bf16[4,256,512]{2,1,0:T(8,128)(2,1)}), bf16[4,256,512]{2,1,0:T(8,128)(2,1)}, u32[]{:S(2)}, u32[]{:S(2)}) async-start(bf16[4,256,512]{2,1,0:T(8,128)(2,1)} %bitcast.149), calls=%async_computation.7 | async-start | bytes 2097152 | tf_op jit(solution)/shard_map/all_to_all | solution.py:70
  476.6 9.1 %copy-start.3 = (bf16[256,512]{1,0:T(8,128)(2,1)S(1)}, bf16[256,512]{1,0:T(8,128)(2,1)}, u32[]{:S(2)}) copy-start(bf16[256,512]{1,0:T(8,128)(2,1)} %copy-done.2) | copy-start | bytes 786436
Sparse Core Ops, SparseCore 0:
  27.3 124.3 all-gather.4
  153.5 73.2 all-gather.6
